TPU v7x, 32 devices: a whole 2x2x4 slice. The times are simulated.
32 devices in a mesh: occ: 4 (over y, x), vir: 8 (over z, core).
Axes of the slice: x: 2, y: 2, z: 4, core: 2. Of those that a mesh axis runs over, the one named last changes fastest.
Arguments:
- amplitudes: bfloat16 [2048, 16384], P('occ', 'vir'), may hold values from -6 to 6
- integrals: bfloat16 [16384, 512], P('vir', 'occ'), may hold values from -0.09375 to 0.09375
- active: int32 [16, 128], P('occ', 'vir'), may hold values from 0 to 1
Outputs:
- residual: bfloat16 [2048, 512], P('occ', 'vir')
All inputs are finite; a program needn't handle non-finite values.
Results may differ from a plain program's by a relative error of at most 0.001.
Values may be sent and summed in bfloat16 or wider, within the bound.
A program may use at most 64 MiB of HBM per device.

v0:
```python
import jax
import jax.numpy as jnp
from jax import lax
from jax.sharding import PartitionSpec as P

TILE = 128


def on_device(amplitudes, integrals, active):
    row_tiles = active.shape[0]
    pair_tiles = active.shape[1]
    row_count = amplitudes.shape[0]
    blocks = amplitudes.reshape(row_tiles, TILE, pair_tiles, TILE)
    masked = (blocks * active.astype(amplitudes.dtype)[:, None, :, None]).reshape(
        row_count, pair_tiles * TILE
    )
    partial_sum = jnp.dot(
        masked,
        lax.all_gather(integrals, "occ", axis=1, tiled=True),
        preferred_element_type=jnp.float32,
    )
    return lax.psum_scatter(partial_sum, "vir", scatter_dimension=1, tiled=True).astype(
        jnp.bfloat16
    )


def solution(mesh):
    return jax.shard_map(
        on_device,
        mesh=mesh,
        in_specs=(P("occ", "vir"), P("vir", "occ"), P("occ", "vir")),
        out_specs=P("occ", "vir"),
        check_vma=False,
    )
```

profile of v0, /device:TPU:6, one launch (start us, length us, event | category | flops | bytes accessed | tf_op | source)
XLA Modules:
  0.0 91.0 jit_solution(10855145946510568011)
XLA Ops:
  6.5 0.0 copy-start
  6.5 0.0 all-gather.2.cloned.1.call-start
  6.5 0.7 all-gather.2.cloned.1.call-update
  7.3 0.0 reduce-scatter.2.cloned.1.call-start
  7.3 0.7 convert_element_type.6
  8.0 36.5 %all-gather.2.cloned.1.call-done = bf16[2048,512]{1,0:T(8,128)(2,1)} async-done(((bf16[2048,128]{1,0:T(8,128)(2,1)}), bf16[2048,512]{1,0:T(8,128)(2,1)}) %all-gather.2.cloned.1.call-update) | async-done | bytes 2097168 | tf_op jit(solution)/shard_map/all_gather | solution.py:19
  44.5 0.3 mul.11
  44.8 0.0 copy-done
  44.9 4.0 %fusion = f32[512,512]{0,1:T(8,128)} fusion(bf16[2048,512]{1,0:T(8,128)(2,1)} %all-gather.2.cloned.1.call-done, bf16[512,2048]{1,0:T(8,128)(2,1)S(1)} %copy-done, bf16[64,8,16,128]{3,2,1,0:T(8,128)(2,1)S(1)} %bitcast.6), kind=kOutput, calls=%fused_computation.1 | convolution fusion | flops 1074790400 | bytes 7340032 | tf_op jit(solution)/shard_map/dot_general | solution.py:17
  48.9 0.0 reduce-scatter.2.cloned.1.call-update
  48.9 33.7 %reduce-scatter.2.cloned.1.call-done = f32[512,64]{0,1:T(8,128)} async-done(((f32[512,512]{0,1:T(8,128)}), f32[512,64]{0,1:T(8,128)}) %reduce-scatter.2.cloned.1.call-update) | async-done | bytes 131088 | tf_op jit(solution)/shard_map/reduce_scatter | solution.py:22
  82.6 1.5 %convert_element_type.7 = bf16[512,64]{0,1:T(8,128)(2,1)} convert(f32[512,64]{0,1:T(8,128)} %reduce-scatter.2.cloned.1.call-done) | non-fusion elementwise | flops 32768 | bytes 196608 | tf_op jit(solution)/shard_map/convert_element_type | solution.py:22
Async XLA Ops:
  6.5 38.3 %copy-start = (bf16[512,2048]{1,0:T(8,128)(2,1)S(1)}, bf16[512,2048]{1,0:T(8,128)(2,1)}, u32[]{:S(2)}) copy-start(bf16[512,2048]{1,0:T(8,128)(2,1)} %param.3) | copy-start | bytes 6291460
  6.5 38.0 %all-gather.2.cloned.1.call-start = ((), (), s32[]{:S(2)}) async-start(), calls=%async_computation.1 | async-start | bytes 2621440 | tf_op jit(solution)/shard_map/all_gather | solution.py:19
  7.3 75.3 %reduce-scatter.2.cloned.1.call-start = ((), (), s32[]{:S(2)}) async-start(), calls=%async_computation.2 | async-start | bytes 1179648 | tf_op jit(solution)/shard_map/reduce_scatter | solution.py:22
Sparse Core Ops, SparseCore 0:
  9.2 35.2 all-gather.1
  49.0 33.5 reduce-scatter.1
where the time goes:
time: 92.7 us; the launch traced here: 91 us
  waiting for transfers between devices  70.9 us (76%)
  between operations  13.4 us (14%)
  matrix products  4.02 us (4%)
  other arithmetic  2.23 us (2%)
    all_gather x1, waiting for transfers between devices, on_device(): lax.all_gather(integrals, 'occ', axis=1, tiled=True)  36.5 us
    reduce_scatter x1, waiting for transfers between devices, on_device(): lax.psum_scatter(partial_sum, 'vir', scatter_dimension=1, tiled=True)  33.7 us
    dot_general x1, matrix products, on_device(): jnp.dot(masked, lax.all_gather(integrals, 'occ', axis=1, tiled=True), pre...  4.02 us
  transfers between devices with their start and end apart: 2, of which 2 were waited for; matrix products, arithmetic and copies ran while one was open for 1% of the time, Pallas kernels for 0%

commit v1 on v0

v1 whole, which is shorter than its diff:
```python
import functools
import math

import jax
import jax.numpy as jnp
from jax import lax
from jax.experimental import pallas as pl
from jax.experimental.pallas import tpu as pltpu
from jax.sharding import PartitionSpec as P

TILE = 128
MESH = pl.DeviceIdType.MESH


def fast_side(count):
    side = math.isqrt(count)
    while count % side:
        side -= 1
    return side


def kernel(
    p, q, nz, active, a_hbm, b_hbm, out, a, b, give, got, zsend, zrecv, total,
    a_sem, b_sem, own_sem, fwd_sem, recv_sem, give_sem, got_sem, zsend_sem, zrecv_sem,
):
    o = lax.axis_index("occ")
    v = lax.axis_index("vir")
    core, z = lax.rem(v, 2), lax.div(v, 2)
    pi, qi = lax.div(o, q), lax.rem(o, q)
    rows, depth = a.shape
    half = depth // 2
    width = b.shape[2]
    halves = (pl.ds(0, half), pl.ds(half, half))
    sibling = (o, v + 1 - 2 * core)

    def occ_at(dp, dq):
        return lax.rem(pi + dp, p) * q + lax.rem(qi + dq, q)

    def slot(dp, dq):
        return (dp % p) * q + dq % q

    a_copy = pltpu.make_async_copy(a_hbm, a, a_sem)
    a_copy.start()
    b_copy = pltpu.make_async_copy(b_hbm, b.at[0], b_sem)
    b_copy.start()

    barrier = pltpu.get_barrier_semaphore()
    peers = [sibling]
    peers += [(occ_at(0, d), v) for d in range(1, q)]
    peers += [(occ_at(d, 0), v) for d in range(1, p)]
    peers += [(o, lax.rem(z + d, nz) * 2 + core) for d in range(1, nz)]
    for peer in peers:
        pl.semaphore_signal(barrier, inc=1, device_id=peer, device_id_type=MESH)
    pl.semaphore_wait(barrier, len(peers))

    sends = []

    def send_own(dp, dq, h):
        copy = pltpu.make_async_remote_copy(
            src_ref=b_hbm.at[halves[h]],
            dst_ref=b.at[slot(-dp, -dq), halves[h]],
            send_sem=own_sem.at[slot(dp, dq), h],
            recv_sem=recv_sem.at[slot(-dp, -dq), h],
            device_id=(occ_at(dp, dq), v),
            device_id_type=MESH,
        )
        copy.start()
        sends.append(copy)

    def forward(sp, sq, dp, dq, h):
        copy = pltpu.make_async_remote_copy(
            src_ref=b.at[slot(sp, sq), halves[h]],
            dst_ref=b.at[slot(sp - dp, sq - dq), halves[h]],
            send_sem=fwd_sem.at[slot(sp + dp, sq + dq), h],
            recv_sem=recv_sem.at[slot(sp - dp, sq - dq), h],
            device_id=(occ_at(dp, dq), v),
            device_id_type=MESH,
        )
        copy.start()
        sends.append(copy)

    def arrived(dp, dq, h):
        place = b.at[slot(dp, dq), halves[h]]
        pltpu.make_async_copy(place, place, recv_sem.at[slot(dp, dq), h]).wait()

    for d in range(1, q):
        send_own(0, d, 0)
    for d in range(1, p):
        send_own(d, 0, 1)
    for d in range(1, q):
        send_own(0, d, 1)
    for d in range(1, p):
        send_own(d, 0, 0)

    a_copy.wait()
    for r in range(rows // TILE):
        for e in range(depth // TILE):
            place = (pl.ds(r * TILE, TILE), pl.ds(e * TILE, TILE))
            weight = active[r, e].astype(jnp.float32)
            a[place] = (a[place].astype(jnp.float32) * weight).astype(a.dtype)

    low = lax.broadcasted_iota(jnp.int32, (rows // 2, width), 1) < width // 2

    def multiply(dp, dq):
        s = slot(dp, dq)
        part = jnp.dot(a[...], b[s], preferred_element_type=jnp.float32)
        top, bottom = part[: rows // 2], part[rows // 2 :]
        for_first = jnp.where(low, top, pltpu.roll(bottom, width // 2, 1))
        for_second = jnp.where(low, pltpu.roll(top, width // 2, 1), bottom)
        first = core == 0
        give[s] = jnp.where(first, for_second, for_first)
        zsend[s] = jnp.where(first, for_first, for_second)
        copy = pltpu.make_async_remote_copy(
            src_ref=give.at[s],
            dst_ref=got.at[s],
            send_sem=give_sem.at[s],
            recv_sem=got_sem.at[s],
            device_id=sibling,
            device_id_type=MESH,
        )
        copy.start()
        return copy

    def z_copy(dp, dq):
        s = slot(dp, dq)
        owner = occ_at(dp, dq)
        place = lax.rem(z - owner + nz, nz)
        return pltpu.make_async_remote_copy(
            src_ref=zsend.at[s],
            dst_ref=zrecv.at[place],
            send_sem=zsend_sem.at[s],
            recv_sem=zrecv_sem.at[place],
            device_id=(o, owner * 2 + core),
            device_id_type=MESH,
        )

    def hand_over(dp, dq, copy):
        s = slot(dp, dq)
        copy.wait()
        owner = occ_at(dp, dq)

        @pl.when(owner == z)
        def _():
            total[...] = zsend[s] + got[s]

        @pl.when(owner != z)
        def _():
            zsend[s] = zsend[s] + got[s]
            z_copy(dp, dq).start()

    b_copy.wait()
    hand_over(0, 0, multiply(0, 0))

    for d in range(1, q):
        arrived(0, d, 0)
        for f in range(1, p):
            forward(0, d, f, 0, 0)
    for d in range(1, p):
        arrived(d, 0, 1)
        for f in range(1, q):
            forward(d, 0, 0, f, 1)

    near = []
    for d in range(1, q):
        arrived(0, d, 1)
        near.append((0, d, multiply(0, d)))
    for d in range(1, p):
        arrived(d, 0, 0)
        near.append((d, 0, multiply(d, 0)))
    for item in near:
        hand_over(*item)
    for dp in range(1, p):
        for dq in range(1, q):
            arrived(dp, dq, 0)
            arrived(dp, dq, 1)
            hand_over(dp, dq, multiply(dp, dq))

    result = total[...]
    for d in range(1, nz):
        pltpu.make_async_copy(zrecv.at[d], zrecv.at[d], zrecv_sem.at[d]).wait()
        result = result + zrecv[d]
    out[: rows // 2] = result[:, : width // 2].astype(out.dtype)
    out[rows // 2 :] = pltpu.roll(result, width // 2, 1)[:, : width // 2].astype(out.dtype)

    for copy in sends:
        copy.wait_send()
    for dp in range(p):
        for dq in range(q):

            @pl.when(occ_at(dp, dq) != z)
            def _():
                z_copy(dp, dq).wait_send()


def on_device(nocc, nvir, amplitudes, integrals, active):
    rows, depth = amplitudes.shape
    width = integrals.shape[1]
    q = fast_side(nocc)
    p = nocc // q
    nz = nvir // 2
    piece = (rows // 2, width)
    f32 = jnp.float32
    any_space = pl.BlockSpec(memory_space=pl.ANY)
    dma = pltpu.SemaphoreType.DMA
    return pl.pallas_call(
        functools.partial(kernel, p, q, nz),
        out_shape=jax.ShapeDtypeStruct((rows, width // 2), jnp.bfloat16),
        in_specs=[pl.BlockSpec(memory_space=pltpu.SMEM), any_space, any_space],
        out_specs=pl.BlockSpec(memory_space=pltpu.VMEM),
        scratch_shapes=[
            pltpu.VMEM((rows, depth), amplitudes.dtype),
            pltpu.VMEM((nocc, depth, width), integrals.dtype),
            pltpu.VMEM((nocc,) + piece, f32),
            pltpu.VMEM((nocc,) + piece, f32),
            pltpu.VMEM((nocc,) + piece, f32),
            pltpu.VMEM((nz,) + piece, f32),
            pltpu.VMEM(piece, f32),
            dma(()), dma(()),
            dma((nocc, 2)), dma((nocc, 2)), dma((nocc, 2)),
            dma((nocc,)), dma((nocc,)), dma((nocc,)), dma((nz,)),
        ],
        compiler_params=pltpu.CompilerParams(collective_id=0, has_side_effects=True),
    )(active, amplitudes, integrals)


def solution(mesh):
    nocc, nvir = mesh.shape["occ"], mesh.shape["vir"]
    return jax.shard_map(
        functools.partial(on_device, nocc, nvir),
        mesh=mesh,
        in_specs=(P("occ", "vir"), P("vir", "occ"), P("occ", "vir")),
        out_specs=P("occ", "vir"),
        check_vma=False,
    )
```

time: 92.7 us -> 37.8 us (0.41); the launches traced: 91 us -> 37.6 us
  waiting for transfers between devices: 70.9 us -> 0 us
  Pallas kernels: 0 us -> 36 us
  between operations: 13.4 us -> 0.01 us
  matrix products: 4.02 us -> 0 us
  other arithmetic: 2.23 us -> 0 us
  local copies, waits for them, and re-layouts: 0.34 us -> 1.62 us
    all_gather x1 -> x0, waiting for transfers between devices: 36.5 us -> none  [on_device(): lax.all_gather(integrals, 'occ', axis=1, tiled=True)]
    pallas_call x0 -> x1, Pallas kernels: none -> 36 us  [on_device(): pl.pallas_call(functools.partial(kernel, p, q, nz), out_shape=jax.ShapeDt...]
    reduce_scatter x1 -> x0, waiting for transfers between devices: 33.7 us -> none  [on_device(): lax.psum_scatter(partial_sum, 'vir', scatter_dimension=1, tiled=True)]
    dot_general x1 -> x0, matrix products: 4.02 us -> none  [on_device(): jnp.dot(masked, lax.all_gather(integrals, 'occ', axis=1, tiled=True), pre...]
    convert_element_type x2 -> x0, other arithmetic: 2.23 us -> none  [the longest x1 1.54 us: on_device(): lax.psum_scatter(partial_sum, 'vir', scatter_dimension=1, tiled=True)]
    pallas_call x0 -> x1, local copies, waits for them, and re-layouts: none -> 1.62 us  [on_device(): pl.pallas_call(functools.partial(kernel, p, q, nz), out_shape=jax.ShapeDt...]
  transfers between devices with their start and end apart: 2 -> 0, of which waited for: 2 -> 0; matrix products, arithmetic and copies ran while one was open for 1% -> 0% of each run, Pallas kernels for 0% -> 0%
where the time goes in v1:
time: 37.8 us; the launch traced here: 37.6 us
  Pallas kernels  36 us (95%)
  local copies, waits for them, and re-layouts  1.62 us (4%)
    pallas_call x1, Pallas kernels, on_device(): pl.pallas_call(functools.partial(kernel, p, q, nz), out_shape=jax.ShapeDt...  36 us
    pallas_call x1, local copies, waits for them, and re-layouts, on_device(): pl.pallas_call(functools.partial(kernel, p, q, nz), out_shape=jax.ShapeDt...  1.62 us

profile of v1, /device:TPU:6, one launch (start us, length us, event | category | flops | bytes accessed | tf_op | source)
XLA Modules:
  0.0 37.6 jit_solution(13222759396281471578)
XLA Ops:
  0.0 36.0 %shard_map.37 = bf16[512,64]{1,0:T(8,128)(2,1)} custom-call(s32[4,16]{1,0:T(4,128)} %active.1, bf16[512,2048]{1,0:T(8,128)(2,1)} %a_hbm.1, bf16[2048,128]{1,0:T(8,128)(2,1)} %b_hbm.1), custom_call_target="tpu_custom_call" | custom-call | tf_op jit(solution)/shard_map/pallas_call | solution.py:205
  36.0 1.6 %copy.4 = bf16[512,64]{0,1:T(8,128)(2,1)} copy(bf16[512,64]{1,0:T(8,128)(2,1)} %shard_map.37) | data formatting | bytes 131072 | tf_op jit(solution)/shard_map/pallas_call | solution.py:205

commit v2 on v0

v2 whole, which is shorter than its diff:
```python
import functools
import math

import jax
import jax.numpy as jnp
from jax import lax
from jax.experimental import pallas as pl
from jax.experimental.pallas import tpu as pltpu
from jax.sharding import PartitionSpec as P

TILE = 128
CHUNKS = 4
MESH = pl.DeviceIdType.MESH


def fast_side(count):
    side = math.isqrt(count)
    while count % side:
        side -= 1
    return side


def kernel(
    p, q, nz, active, a_hbm, b_hbm, out, a, raw, b, part, got, zsend, zrecv,
    a_sem, b_sem, own_sem, fwd_sem, recv_sem, give_sem, got_sem, zsend_sem, zrecv_sem, reach_sem,
):
    o = lax.axis_index("occ")
    v = lax.axis_index("vir")
    core, z = lax.rem(v, 2), lax.div(v, 2)
    pi, qi = lax.div(o, q), lax.rem(o, q)
    rows, depth = a.shape
    width = raw.shape[1]
    sub = width // CHUNKS
    deep = depth // CHUNKS
    tall = rows // CHUNKS
    short = tall // 2
    per_core = CHUNKS // 2
    halves = (pl.ds(0, deep // 2), pl.ds(deep // 2, deep // 2))
    sibling = (o, v + 1 - 2 * core)
    below, above = (o, v - 2), (o, v + 2)
    f32 = jnp.float32

    def occ_at(dp, dq):
        return lax.rem(pi + dp, p) * q + lax.rem(qi + dq, q)

    def slot(dp, dq):
        return (dp % p) * q + dq % q

    def signal(sem, peer):
        pl.semaphore_signal(sem, inc=1, device_id=peer, device_id_type=MESH)

    b_copy = pltpu.make_async_copy(b_hbm, raw, b_sem)
    b_copy.start()
    a_copy = pltpu.make_async_copy(a_hbm, a, a_sem)
    a_copy.start()

    barrier = pltpu.get_barrier_semaphore()
    near = [sibling]
    near += [(occ_at(0, d), v) for d in range(1, q)]
    near += [(occ_at(d, 0), v) for d in range(1, p)]
    for peer in near:
        signal(barrier, peer)
    pl.when(z > 0)(lambda: signal(barrier, below))
    pl.when(z < nz - 1)(lambda: signal(barrier, above))

    def group_of(shape):
        return lax.div(lax.broadcasted_iota(jnp.int32, shape, 1), sub)

    b_copy.wait()
    group = group_of((deep, width))
    quarters = [raw[k * deep : (k + 1) * deep].astype(f32) for k in range(CHUNKS)]
    for j in range(CHUNKS):
        packed = None
        for k in range(CHUNKS):
            turn = (sub * (k - j)) % width
            piece = pltpu.roll(quarters[k], turn, 1) if turn else quarters[k]
            packed = piece if packed is None else jnp.where(group == k, piece, packed)
        b[0, j] = packed.astype(b.dtype)

    beside = lax.div(z + nz - 1, nz) + lax.div(2 * nz - 2 - z, nz)
    pl.semaphore_wait(barrier, len(near) + beside)

    sends = []

    def remote(src, dst, send_sem, to_sem, peer):
        copy = pltpu.make_async_remote_copy(
            src_ref=src, dst_ref=dst, send_sem=send_sem, recv_sem=to_sem,
            device_id=peer, device_id_type=MESH,
        )
        copy.start()
        return copy

    def send_own(j, stage):
        if j >= CHUNKS:
            return
        moves = [(0, d, stage) for d in range(1, q)] + [(d, 0, 1 - stage) for d in range(1, p)]
        for dp, dq, h in moves:
            s = slot(-dp, -dq)
            sends.append(
                remote(
                    b.at[0, j, halves[h]], b.at[s, j, halves[h]],
                    own_sem.at[s, j, h], recv_sem.at[s, j, h], (occ_at(dp, dq), v),
                )
            )

    def forward(sp, sq, dp, dq, j, h):
        s, t = slot(sp, sq), slot(sp - dp, sq - dq)
        sends.append(
            remote(
                b.at[s, j, halves[h]], b.at[t, j, halves[h]],
                fwd_sem.at[t, j, h], recv_sem.at[t, j, h], (occ_at(dp, dq), v),
            )
        )

    def arrived(dp, dq, j, h):
        s = slot(dp, dq)
        place = b.at[s, j, halves[h]]
        pltpu.make_async_copy(place, place, recv_sem.at[s, j, h]).wait()

    def reach(step):
        pl.when(z > 0)(lambda: signal(reach_sem.at[step, 1], below))
        pl.when(z < nz - 1)(lambda: signal(reach_sem.at[step, 0], above))

    def reached(step):
        pl.when(z > 0)(lambda: pl.semaphore_wait(reach_sem.at[step, 0], 1))
        pl.when(z < nz - 1)(lambda: pl.semaphore_wait(reach_sem.at[step, 1], 1))

    send_own(0, 0)
    send_own(0, 1)
    send_own(1, 0)
    reach(0)

    a_copy.wait()
    for r in range(rows // TILE):
        for e in range(depth // TILE):
            place = (pl.ds(r * TILE, TILE), pl.ds(e * TILE, TILE))
            weight = active[r, e].astype(f32)
            a[place] = (a[place].astype(f32) * weight).astype(a.dtype)

    for step in range(1, nz - 1):
        reached(step - 1)
        reach(step)
    lanes = group_of((tall, width))

    def multiply(dp, dq, j):
        s = slot(dp, dq)
        block = b[s, j]
        parts = [
            jnp.dot(a[:, k * deep : (k + 1) * deep], block, preferred_element_type=f32)
            for k in range(CHUNKS)
        ]
        summed = None
        for d in range(CHUNKS):
            mixed = None
            for k in range(CHUNKS):
                r = (k + d) % CHUNKS
                piece = parts[k][r * tall : (r + 1) * tall]
                mixed = piece if mixed is None else jnp.where(lanes == k, piece, mixed)
            mixed = pltpu.roll(mixed, sub * d, 1) if d else mixed
            summed = mixed if summed is None else summed + mixed
        part[s, j, 0] = summed[:short]
        part[s, j, 1] = summed[short:]
        copy = remote(
            part.at[s, j, 1 - core], got.at[s, j], give_sem.at[s, j], got_sem.at[s, j], sibling
        )
        return dp, dq, j, copy

    def z_copy(dp, dq, j):
        s = slot(dp, dq)
        owner = occ_at(dp, dq)
        place = lax.rem(z - owner + nz, nz)
        keeper = j // per_core
        return pltpu.make_async_remote_copy(
            src_ref=zsend.at[s, j],
            dst_ref=zrecv.at[j % per_core, place, core],
            send_sem=zsend_sem.at[s, j],
            recv_sem=zrecv_sem.at[j % per_core, place, core],
            device_id=(o, owner * 2 + keeper),
            device_id_type=MESH,
        )

    def stays(dp, dq, j):
        return occ_at(dp, dq) * 2 + j // per_core == v

    def hand_over(dp, dq, j, copy):
        s = slot(dp, dq)
        copy.wait()
        value = part[s, j, core] + got[s, j]

        @pl.when(stays(dp, dq, j))
        def _():
            zrecv[j % per_core, 0, core] = value

        @pl.when(jnp.logical_not(stays(dp, dq, j)))
        def _():
            zsend[s, j] = value
            z_copy(dp, dq, j).start()

    pending = []

    def run(dp, dq, j):
        pending.append(multiply(dp, dq, j))
        while len(pending) > 1:
            hand_over(*pending.pop(0))

    def diagonals(j):
        for dp in range(1, p):
            for dq in range(1, q):
                arrived(dp, dq, j, 0)
                arrived(dp, dq, j, 1)
                run(dp, dq, j)

    first = multiply(0, 0, 0)
    pending.append(first)
    reached(nz - 2)
    for j in range(CHUNKS):
        for d in range(1, q):
            arrived(0, d, j, 0)
            for f in range(1, p):
                forward(0, d, f, 0, j, 0)
        for d in range(1, p):
            arrived(d, 0, j, 1)
            for f in range(1, q):
                forward(d, 0, 0, f, j, 1)
        send_own(j + 1, 1)
        send_own(j + 2, 0)
        if j:
            diagonals(j - 1)
        if j + 1 < CHUNKS:
            run(0, 0, j + 1)
        for d in range(1, q):
            arrived(0, d, j, 1)
            run(0, d, j)
        for d in range(1, p):
            arrived(d, 0, j, 0)
            run(d, 0, j)
    while pending:
        hand_over(*pending.pop(0))
    diagonals(CHUNKS - 1)
    while pending:
        hand_over(*pending.pop(0))

    sums = {}
    for g in range(per_core):
        for k in range(2):
            for d in range(nz):

                def wait(g=g, d=d, k=k):
                    place = zrecv.at[g, d, k]
                    pltpu.make_async_copy(place, place, zrecv_sem.at[g, d, k]).wait()

                if d:
                    wait()
                else:
                    pl.when(core != k)(wait)
            total = zrecv[g, 0, k]
            for d in range(1, nz):
                total = total + zrecv[g, d, k]
            sums[g, k] = total
    small = group_of((short, width))
    for r in range(CHUNKS):
        for k in range(2):
            value = None
            for g in range(per_core):
                turn = (sub * (g - r)) % width
                piece = pltpu.roll(sums[g, k], turn, 1) if turn else sums[g, k]
                value = piece if value is None else jnp.where(small == g, piece, value)
            start = r * tall + k * short
            out[start : start + short] = value[:, : width // 2].astype(out.dtype)

    for copy in sends:
        copy.wait_send()
    for j in range(CHUNKS):
        for dp in range(p):
            for dq in range(q):

                @pl.when(jnp.logical_not(stays(dp, dq, j)))
                def _():
                    z_copy(dp, dq, j).wait_send()


def on_device(nocc, nvir, amplitudes, integrals, active):
    rows, depth = amplitudes.shape
    width = integrals.shape[1]
    q = fast_side(nocc)
    p = nocc // q
    nz = nvir // 2
    g = CHUNKS
    short = rows // g // 2
    f32 = jnp.float32
    any_space = pl.BlockSpec(memory_space=pl.ANY)
    dma = pltpu.SemaphoreType.DMA
    return pl.pallas_call(
        functools.partial(kernel, p, q, nz),
        out_shape=jax.ShapeDtypeStruct((rows, width // 2), jnp.bfloat16),
        in_specs=[pl.BlockSpec(memory_space=pltpu.SMEM), any_space, any_space],
        out_specs=pl.BlockSpec(memory_space=pltpu.VMEM),
        scratch_shapes=[
            pltpu.VMEM((rows, depth), amplitudes.dtype),
            pltpu.VMEM((depth, width), integrals.dtype),
            pltpu.VMEM((nocc, g, depth // g, width), integrals.dtype),
            pltpu.VMEM((nocc, g, 2, short, width), f32),
            pltpu.VMEM((nocc, g, short, width), f32),
            pltpu.VMEM((nocc, g, short, width), f32),
            pltpu.VMEM((g // 2, nz, 2, short, width), f32),
            dma(()), dma(()),
            dma((nocc, g, 2)), dma((nocc, g, 2)), dma((nocc, g, 2)),
            dma((nocc, g)), dma((nocc, g)), dma((nocc, g)), dma((g // 2, nz, 2)),
            pltpu.SemaphoreType.REGULAR((nz - 1, 2)),
        ],
        compiler_params=pltpu.CompilerParams(collective_id=0, has_side_effects=True),
    )(active, amplitudes, integrals)


def solution(mesh):
    nocc, nvir = mesh.shape["occ"], mesh.shape["vir"]
    return jax.shard_map(
        functools.partial(on_device, nocc, nvir),
        mesh=mesh,
        in_specs=(P("occ", "vir"), P("vir", "occ"), P("occ", "vir")),
        out_specs=P("occ", "vir"),
        check_vma=False,
    )
```

time: 92.7 us -> 32.9 us (0.35)
  the two profiles are of different devices: /device:TPU:6 before, /device:TPU:13 now
where the time goes in v2:
time: 32.9 us; the launch traced here: 32.7 us
  Pallas kernels  31.1 us (95%)
  local copies, waits for them, and re-layouts  1.62 us (5%)
    pallas_call x1, Pallas kernels, on_device(): pl.pallas_call(functools.partial(kernel, p, q, nz), out_shape=jax.ShapeDt...  31.1 us
    pallas_call x1, local copies, waits for them, and re-layouts, on_device(): pl.pallas_call(functools.partial(kernel, p, q, nz), out_shape=jax.ShapeDt...  1.62 us

profile of v2, /device:TPU:13, one launch (start us, length us, event | category | flops | bytes accessed | tf_op | source)
XLA Modules:
  0.0 32.7 jit_solution(4243669202297214545)
XLA Ops:
  0.0 31.1 %shard_map.37 = bf16[512,64]{1,0:T(8,128)(2,1)} custom-call(s32[4,16]{1,0:T(4,128)} %active.1, bf16[512,2048]{1,0:T(8,128)(2,1)} %a_hbm.1, bf16[2048,128]{1,0:T(8,128)(2,1)} %b_hbm.1), custom_call_target="tpu_custom_call" | custom-call | tf_op jit(solution)/shard_map/pallas_call | solution.py:293
  31.1 1.6 %copy.4 = bf16[512,64]{0,1:T(8,128)(2,1)} copy(bf16[512,64]{1,0:T(8,128)(2,1)} %shard_map.37) | data formatting | bytes 131072 | tf_op jit(solution)/shard_map/pallas_call | solution.py:293
